TPU v7x, 32 devices: a whole 2x2x4 slice. The times are simulated.
32 devices in a mesh: groups: 2 (over x), seq: 8 (over z, y), pipe: 2 (over core).
Axes of the slice: x: 2, y: 2, z: 4, core: 2. Of those that a mesh axis runs over, the one named last changes fastest.
Arguments:
- tokens: bfloat16 [2, 2048, 1440], P('pipe', ('groups', 'seq')), parts along dimension 1, may hold values from -6 to 6
- routes: int32 [2, 2048, 4], P('pipe', ('groups', 'seq')), parts along dimension 1, may hold values from 0 to 15, all different within a row; in each aligned block of 128 rows (0 to 127, 128 to 255, ..., all dimensions but the last counted through in order) at most 48 rows name the same one
- route_weights: float32 [2, 2048, 4], P('pipe', ('groups', 'seq')), parts along dimension 1, may hold values from 0.1 to 1
- moe_gain: float32 [1440], replicated, may hold values from 0.5 to 1.5
- gate_up: bfloat16 [32, 1440, 1440], P('seq'), may hold values from -0.15625 to 0.15625
- down_proj: bfloat16 [32, 720, 1440], P('seq'), may hold values from -0.15625 to 0.15625
- attn_gain: float32 [1440], replicated, may hold values from 0.5 to 1.5
- qkv_proj: bfloat16 [1440, 2560], P('seq'), may hold values from -0.15625 to 0.15625
- head_sink_logits: float32 [32], replicated, may hold values from 3 to 6
- out_proj: bfloat16 [2048, 1440], P('seq'), may hold values from -0.125 to 0.125
Outputs:
- layer_output: bfloat16 [2, 2048, 1440], P('pipe', ('groups', 'seq')), parts along dimension 1
There are 2 independent parts, one for each index of `groups`. A program takes and returns all parts, laid end to end along the dimension named above; an argument that names none is the same for every part. Nothing has to cross between parts.
Inputs may be any that keep to these rules, and one draw needn't show every extreme that they name: `routes`: within the 128 positions of one micro-batch on one index of seq, a token names each of its 4 experts once, and each expert is named by at most 48 tokens; one expert is named by exactly 48 of them.
All inputs are finite; a program needn't handle non-finite values.
Results may differ from a plain program's by a relative error of at most 0.0085.
Values may be sent and summed in bfloat16 or wider, within the bound.
A program may use at most 128 MiB of HBM per device.

v0:
```python
import jax
import jax.numpy as jnp
from jax import lax
from jax.sharding import PartitionSpec as P

E = 16
TOP = 4
QUERY_HEADS = 32
KEY_VALUE_HEADS = 4
HEAD_SIZE = 64
WINDOW_SPAN = 128
HALF = 720
CAP = 48


eps = 1e-05


def from_partner(value, axis, distance):
    return lax.ppermute(value, axis, [(i, i ^ 1 << distance) for i in range(lax.axis_size(axis))])


def shifted(value, axis, steps):
    count = lax.axis_size(axis)
    pairs = [(source, (source + steps) % count) for source in range(count)]
    return lax.ppermute(value, axis, pairs)


def passed_along(value, axis, steps):
    count = lax.axis_size(axis)
    first, last = (max(0, -steps), min(count, count - steps))
    return lax.ppermute(value, axis, [(source, source + steps) for source in range(first, last)])


def rms_scale(value_matrix, gain):
    widened = value_matrix.astype(jnp.float32)
    mean_square = jnp.mean(widened * widened, axis=-1, keepdims=True)
    return (widened * lax.rsqrt(mean_square + eps) * gain).astype(jnp.bfloat16)


def slot_positions(route_rows):
    flat = route_rows.reshape(-1)
    onehot = (flat[:, None] == jnp.arange(E, dtype=jnp.int32)[None, :]).astype(jnp.int32)
    earlier = jnp.cumsum(onehot, axis=0) - onehot
    return flat * CAP + jnp.sum(earlier * onehot, axis=1)


def expert_layer(local, route_rows, route_scale, moe_gain, gate_up, down_proj):
    tok_count, width = local.shape
    seq_count = lax.axis_size("seq")
    per_device = gate_up.shape[0]
    normed = rms_scale(local, moe_gain)
    positions = slot_positions(route_rows)
    select = (positions[None, :] == jnp.arange(E * CAP, dtype=jnp.int32)[:, None]).astype(
        jnp.bfloat16
    )
    repeated = jnp.repeat(normed, TOP, axis=0)
    table = jnp.dot(select, repeated, preferred_element_type=jnp.float32).astype(jnp.bfloat16)
    by_expert = table.reshape(E, CAP, width)
    first = lax.axis_index("seq") % 2 == 0
    outgoing = jnp.repeat(by_expert, 2, axis=0).reshape(seq_count, per_device, CAP, width)
    received = lax.all_to_all(outgoing, "seq", split_axis=0, concat_axis=0, tiled=True)
    projected = jnp.einsum("spcd,pdh->spch", received, gate_up, preferred_element_type=jnp.float32)
    gate_part = projected[..., :HALF]
    up_part = projected[..., HALF:]
    hidden = (gate_part * jax.nn.sigmoid(1.702 * gate_part) * (up_part + 1.0)).astype(jnp.bfloat16)
    partial_value = jnp.einsum(
        "spch,phd->spcd", hidden, down_proj, preferred_element_type=jnp.float32
    )
    if per_device >= 2:
        finished = (
            partial_value.reshape(seq_count, per_device // 2, 2, CAP, width)
            .sum(axis=2)
            .astype(jnp.bfloat16)
        )
    else:
        lower_rows = partial_value[:, :, : CAP // 2]
        upper_rows = partial_value[:, :, CAP // 2 :]
        kept = jnp.where(first, lower_rows, upper_rows)
        given = jnp.where(first, upper_rows, lower_rows)
        partner_part = from_partner(given.astype(jnp.bfloat16), "seq", 0).astype(given.dtype)
        finished = (kept + partner_part).astype(jnp.bfloat16)
    summed = lax.all_to_all(finished, "seq", split_axis=0, concat_axis=0, tiled=True).reshape(
        E * CAP, width
    )
    picked = lax.dot_general(
        select, summed, (((0,), (0,)), ((), ())), preferred_element_type=jnp.float32
    )
    weighted = jnp.sum(picked.reshape(tok_count, TOP, width) * route_scale[:, :, None], axis=1)
    return (local.astype(jnp.float32) + weighted).astype(jnp.bfloat16)


def attend(query_matrix, keys_extended, values_extended, head_sink_logits, halo_valid):
    tok_count = query_matrix.shape[0]
    query_groups = QUERY_HEADS // KEY_VALUE_HEADS
    attention_block = min(tok_count, 512)
    scale = float(HEAD_SIZE) ** (-0.5)
    sink_mass_total = jnp.exp(head_sink_logits).reshape(KEY_VALUE_HEADS, query_groups, 1, 1)
    block_queries = query_matrix.reshape(attention_block, KEY_VALUE_HEADS, query_groups, HEAD_SIZE)
    block_keys = keys_extended.reshape(attention_block + WINDOW_SPAN, KEY_VALUE_HEADS, HEAD_SIZE)
    block_values = values_extended.reshape(
        attention_block + WINDOW_SPAN, KEY_VALUE_HEADS, HEAD_SIZE
    )
    scores = (
        jnp.einsum("qhgd,khd->hgqk", block_queries, block_keys, preferred_element_type=jnp.float32)
        * scale
    )
    query_pos = jnp.arange(attention_block, dtype=jnp.int32)[:, None] + WINDOW_SPAN
    key_pos = jnp.arange(attention_block + WINDOW_SPAN, dtype=jnp.int32)[None, :]
    distance = query_pos - key_pos
    allowed = (
        (distance >= 0) & (distance < WINDOW_SPAN) & ((key_pos + 0 >= WINDOW_SPAN) | halo_valid)
    )
    weights = jnp.where(allowed, jnp.exp(scores), 0.0)
    probs = (weights / (jnp.sum(weights, axis=-1, keepdims=True) + sink_mass_total)).astype(
        jnp.bfloat16
    )
    mixed = jnp.einsum("hgqk,khd->qhgd", probs, block_values, preferred_element_type=jnp.float32)
    outputs = mixed.reshape(attention_block, QUERY_HEADS * HEAD_SIZE).astype(jnp.bfloat16)
    return outputs


def body(
    tokens,
    routes,
    route_weights,
    moe_gain,
    gate_up,
    down_proj,
    attn_gain,
    qkv_proj,
    head_sink_logits,
    out_proj,
):
    hidden = expert_layer(tokens[0], routes[0], route_weights[0], moe_gain, gate_up, down_proj)
    tok_count, width = hidden.shape
    normed = rms_scale(hidden, attn_gain)
    seq_index = lax.axis_index("seq")
    pipe_index = lax.axis_index("pipe")
    halo_valid = (seq_index > 0) | (pipe_index > 0)
    query_width = QUERY_HEADS * HEAD_SIZE
    width_of_pair = KEY_VALUE_HEADS * HEAD_SIZE
    columns = normed
    packed_heads = jnp.dot(
        columns,
        lax.all_gather(qkv_proj, "seq", axis=0, tiled=True),
        preferred_element_type=jnp.float32,
    ).astype(jnp.bfloat16)
    from_left = shifted(packed_heads[tok_count - WINDOW_SPAN :, query_width:], "seq", 1)
    from_section = passed_along(from_left, "pipe", 1)
    halo_pairs = jnp.where(seq_index == 0, from_section, from_left)
    query_matrix = packed_heads[:, :query_width]
    pairs_ext = jnp.concatenate([halo_pairs, packed_heads[:, query_width:]], axis=0)
    keys_extended = pairs_ext[:, :width_of_pair]
    values_extended = pairs_ext[:, width_of_pair:]
    attended = attend(query_matrix, keys_extended, values_extended, head_sink_logits, halo_valid)
    columns = attended
    projected = jnp.dot(
        columns,
        lax.all_gather(out_proj, "seq", axis=0, tiled=True),
        preferred_element_type=jnp.float32,
    )
    return (hidden.astype(jnp.float32) + projected).astype(jnp.bfloat16)[None]


def solution(mesh):
    in_specs = (
        P("pipe", ("groups", "seq"), None),
        P("pipe", ("groups", "seq"), None),
        P("pipe", ("groups", "seq"), None),
        P(),
        P("seq", None, None),
        P("seq", None, None),
        P(),
        P("seq", None),
        P(),
        P("seq", None),
    )
    out_specs = P("pipe", ("groups", "seq"), None)
    return jax.shard_map(body, mesh=mesh, in_specs=in_specs, out_specs=out_specs, check_vma=False)
```

profile of v0, /device:TPU:0, one launch (start us, length us, event | category | flops | bytes accessed | tf_op | source)
XLA Modules:
  0.0 386.2 jit_solution(929708166712406774)
XLA Ops:
  6.5 0.0 all-gather.6.cloned.1.call-start
  6.5 0.7 all-gather.6.cloned.1.call-update
  7.3 0.8 copy.44
  8.0 0.1 eq.61
  8.2 0.1 reshape_squeeze.3
  8.3 1.2 reduce-window.6
  9.4 0.2 slice_reduce_fusion
  9.7 1.2 fusion.32
  10.9 1.2 fusion.34
  12.1 0.2 copy.49
  12.3 0.4 broadcast_in_dim.12
  12.8 0.8 reshape.112
  13.5 0.1 fusion.46
  13.6 2.8 convolution_convert_fusion.1
  16.4 2.8 copy.50
  19.2 2.7 broadcast_in_dim.15
  21.9 7.4 %all-to-all-start = ((bf16[8,4,48,1440]{3,2,1,0:T(8,128)(2,1)}), bf16[8,4,48,1440]{3,2,1,0:T(8,128)(2,1)}, u32[]{:S(2)}, u32[]{:S(2)}) async-start(bf16[8,4,48,1440]{3,2,1,0:T(8,128)(2,1)} %bitcast.92), calls=%async_computation | async-start | bytes 9437184 | tf_op jit(solution)/shard_map/all_to_all | solution.py:62
  29.3 0.0 all-gather.4.cloned.1.call-start
  29.4 0.7 all-gather.4.cloned.1.call-update
  30.1 181.4 %all-to-all-done = bf16[8,4,48,1440]{3,2,1,0:T(8,128)(2,1)} async-done(((bf16[8,4,48,1440]{3,2,1,0:T(8,128)(2,1)}), bf16[8,4,48,1440]{3,2,1,0:T(8,128)(2,1)}, u32[]{:S(2)}, u32[]{:S(2)}) %all-to-all-start) | async-done | bytes 4423712 | tf_op jit(solution)/shard_map/all_to_all | solution.py:62
  211.5 16.6 %fusion.4 = f32[8,4,48,1440]{3,2,0,1:T(8,128)} fusion(bf16[4,1440,1440]{2,1,0:T(8,128)(2,1)} %param.14, bf16[8,4,48,1440]{3,2,1,0:T(8,128)(2,1)} %all-to-all-done), kind=kOutput, calls=%fused_computation.5 | convolution fusion | flops 6370099200 | bytes 29859840 | tf_op jit(solution)/shard_map/spcd,pdh->spch/dot_general | solution.py:63
  228.2 10.8 %bitcast_reduce_fusion = bf16[8,2,48,1440]{3,2,0,1:T(8,128)(2,1)S(1)} fusion(bf16[4,720,1440]{2,1,0:T(8,128)(2,1)} %param.15, f32[8,4,48,1440]{3,2,0,1:T(8,128)} %fusion.4), kind=kOutput, calls=%fused_computation.2 | convolution fusion | flops 3195002880 | bytes 19353600 | tf_op jit(solution)/shard_map/spch,phd->spcd/dot_general | solution.py:67
  238.9 0.0 copy-start.2
  238.9 1.6 copy.52
  240.6 8.9 %all-to-all-start.1 = ((bf16[8,2,48,1440]{3,2,1,0:T(8,128)(2,1)}), bf16[8,2,48,1440]{3,2,1,0:T(8,128)(2,1)S(1)}, u32[]{:S(2)}, u32[]{:S(2)}) async-start(bf16[8,2,48,1440]{3,2,1,0:T(8,128)(2,1)} %copy.52), calls=%async_computation.1 | async-start | bytes 4718592 | tf_op jit(solution)/shard_map/all_to_all | solution.py:83
  249.4 0.1 reduce_sum.57
  249.6 0.1 copy.48
  249.6 99.0 %all-to-all-done.1 = bf16[8,2,48,1440]{3,2,1,0:T(8,128)(2,1)S(1)} async-done(((bf16[8,2,48,1440]{3,2,1,0:T(8,128)(2,1)}), bf16[8,2,48,1440]{3,2,1,0:T(8,128)(2,1)S(1)}, u32[]{:S(2)}, u32[]{:S(2)}) %all-to-all-start.1) | async-done | bytes 2211872 | tf_op jit(solution)/shard_map/all_to_all | solution.py:83
  348.6 1.5 fusion.23
  350.1 0.0 copy-done
  350.1 0.2 fusion.29
  350.3 0.0 all-gather.6.cloned.1.call-done
  350.4 7.0 %reshape.121 = bf16[1440,2560]{1,0:T(8,128)(2,1)} reshape(bf16[8,180,2560]{2,1,0:T(8,128)(2,1)} %all-gather.6.cloned.1.call-done) | data formatting | bytes 14745600
  357.4 4.4 %convolution_convert_fusion = bf16[128,2560]{1,0:T(8,128)(2,1)S(1)} fusion(bf16[1440,2560]{1,0:T(8,128)(2,1)} %reshape.121, bf16[128,1440]{0,1:T(8,128)(2,1)S(1)} %get-tuple-element.6, f32[1440]{0:T(1024)S(1)} %copy-done.1, f32[128]{0:T(128)S(1)} %add_rsqrt_fusion), kind=kOutput, calls=%fused_computation.12 | convolution fusion | flops 944783360 | bytes 8403072 | tf_op jit(solution)/shard_map/dot_general | solution.py:144
  361.8 1.1 collective-permute-start
  362.9 0.1 add.73
  363.0 6.5 %collective-permute-done = bf16[128,512]{1,0:T(8,128)(2,1)S(1)} collective-permute-done((bf16[128,512]{1,0:T(8,128)(2,1)S(1)}, bf16[128,512]{1,0:T(8,128)(2,1)S(1)}, u32[]{:S(2)}, u32[]{:S(2)}) %collective-permute-start) | collective-permute-done | bytes 131104 | tf_op jit(solution)/shard_map/ppermute | solution.py:26
  369.5 1.3 collective-permute-start.1
  370.8 0.1 fusion.43
  371.0 0.3 copy.56
  371.2 0.5 collective-permute-done.1
  371.8 0.1 copy.55
  371.9 0.1 copy.54
  372.0 1.0 fusion.10
  373.1 0.1 broadcast_add_fusion
  373.1 1.0 fusion.26
  374.2 0.0 all-gather.4.cloned.1.call-done
  374.2 5.1 %fusion.15 = bf16[1,128,1440]{1,2,0:T(8,128)(2,1)} fusion(bf16[2048,1440]{0,1:T(8,128)(2,1)} %all-gather.4.cloned.1.call-done, bf16[128,2048]{0,1:T(8,128)(2,1)S(1)} %bitcast.100, bf16[128,1440]{0,1:T(8,128)(2,1)S(1)} %get-tuple-element.6), kind=kOutput, calls=%fused_computation.20 | convolution fusion | flops 755527680 | bytes 7159808 | tf_op jit(solution)/shard_map/dot_general | solution.py:158
  (20 shorter events, 0.2 us)
Async XLA Ops:
  6.5 343.8 %all-gather.6.cloned.1.call-start = ((), (), s32[]{:S(2)}) async-start(), calls=%async_computation.3 | async-start | bytes 8478720 | tf_op jit(solution)/shard_map/all_gather | solution.py:146
  21.9 189.6 %all-to-all-start = ((bf16[8,4,48,1440]{3,2,1,0:T(8,128)(2,1)}), bf16[8,4,48,1440]{3,2,1,0:T(8,128)(2,1)}, u32[]{:S(2)}, u32[]{:S(2)}) async-start(bf16[8,4,48,1440]{3,2,1,0:T(8,128)(2,1)} %bitcast.92), calls=%async_computation | async-start | bytes 9437184 | tf_op jit(solution)/shard_map/all_to_all | solution.py:62
  29.3 344.9 %all-gather.4.cloned.1.call-start = ((), (), s32[]{:S(2)}) async-start(), calls=%async_computation.2 | async-start | bytes 6635520 | tf_op jit(solution)/shard_map/all_gather | solution.py:160
  238.9 109.7 %copy-start.2 = (f32[1,128,4]{1,2,0:T(4,128)S(1)}, f32[1,128,4]{1,2,0:T(4,128)}, u32[]{:S(2)}) copy-start(f32[1,128,4]{1,2,0:T(4,128)} %param.12) | copy-start | bytes 6148
  240.6 108.1 %all-to-all-start.1 = ((bf16[8,2,48,1440]{3,2,1,0:T(8,128)(2,1)}), bf16[8,2,48,1440]{3,2,1,0:T(8,128)(2,1)S(1)}, u32[]{:S(2)}, u32[]{:S(2)}) async-start(bf16[8,2,48,1440]{3,2,1,0:T(8,128)(2,1)} %copy.52), calls=%async_computation.1 | async-start | bytes 4718592 | tf_op jit(solution)/shard_map/all_to_all | solution.py:83
  249.4 100.7 %copy-start = (bf16[1,128,1440]{1,2,0:T(8,128)(2,1)S(1)}, bf16[1,128,1440]{1,2,0:T(8,128)(2,1)}, u32[]{:S(2)}) copy-start(bf16[1,128,1440]{1,2,0:T(8,128)(2,1)} %param.10) | copy-start | bytes 1105924
  350.3 7.0 %copy-start.1 = (f32[1440]{0:T(1024)S(1)}, f32[1440]{0:T(1024)}, u32[]{:S(2)}) copy-start(f32[1440]{0:T(1024)} %param.16) | copy-start | bytes 17284
  357.4 5.5 %copy-start.3 = (f32[32]{0:T(128)S(1)}, f32[32]{0:T(128)}, u32[]{:S(2)}) copy-start(f32[32]{0:T(128)} %param.18) | copy-start | bytes 388
  361.8 7.7 %collective-permute-start = (bf16[128,512]{1,0:T(8,128)(2,1)S(1)}, bf16[128,512]{1,0:T(8,128)(2,1)S(1)}, u32[]{:S(2)}, u32[]{:S(2)}) collective-permute-start(bf16[128,512]{1,0:T(8,128)(2,1)S(1)} %slice.36), channel_id=1, source_target_pairs={{0,2},{2,4},{4,6},{6,8},{8,10},{10,12},{12,14},{14,0},{1,3},{3,5},... | collective-permute-start | bytes 393224 | tf_op jit(solution)/shard_map/ppermute | solution.py:26
  369.5 2.3 collective-permute-start.1
Sparse Core Ops, SparseCore 0:
  9.5 207.8 all-gather.5
  219.5 134.6 all-gather.3
where the time goes:
time: 387 us; the launch traced here: 386 us
  waiting for transfers between devices  289 us (75%)
  matrix products  43.3 us (11%)
  starting transfers between devices  18.7 us (5%)
  local copies, waits for them, and re-layouts  17.5 us (5%)
  between operations  13.6 us (4%)
  other arithmetic  4.21 us (1%)
    all_to_all x1, waiting for transfers between devices, expert_layer(): lax.all_to_all(outgoing, 'seq', split_axis=0, concat_axis=0, tiled=True)  181 us
    all_to_all x1, waiting for transfers between devices, expert_layer(): lax.all_to_all(finished, 'seq', split_axis=0, concat_axis=0, tiled=True)  99 us
    dot_general x1, matrix products, expert_layer(): jnp.einsum('spcd,pdh->spch', received, gate_up, preferred_element_type=jn...  16.6 us
    dot_general x1, matrix products, expert_layer(): jnp.einsum('spch,phd->spcd', hidden, down_proj, preferred_element_type=jn...  10.8 us
    all_to_all x1, starting transfers between devices, expert_layer(): lax.all_to_all(finished, 'seq', split_axis=0, concat_axis=0, tiled=True)  8.86 us
    unnamed x10, local copies, waits for them, and re-layouts  7.8 us
  transfers between devices with their start and end apart: 6, of which 4 were waited for; matrix products, arithmetic and copies ran while one was open for 15% of the time, Pallas kernels for 0%

commit v1 on v0

--- a/solution.py
+++ b/solution.py
@@ -1,8 +1,13 @@
+import functools
+
 import jax
 import jax.numpy as jnp
 from jax import lax
+from jax.experimental import pallas as pl
+from jax.experimental.pallas import tpu as pltpu
 from jax.sharding import PartitionSpec as P
 
+MESH = pl.DeviceIdType.MESH
 E = 16
 TOP = 4
 QUERY_HEADS = 32
@@ -163,6 +168,250 @@
     return (hidden.astype(jnp.float32) + projected).astype(jnp.bfloat16)[None]
 
 
+def ring_place(index, count, folded):
+    if not folded:
+        return index
+    line, side = index // 2, index % 2
+    return line + side * (count - 1 - 2 * line)
+
+def ring_index(place, count, folded):
+    if not folded:
+        return place
+    side = place // (count // 2)
+    line = place + side * (count - 1 - 2 * place)
+    return 2 * line + side
+
+def greet(peers):
+    barrier = pltpu.get_barrier_semaphore()
+    for peer in peers:
+        pl.semaphore_signal(barrier, inc=1, device_id={"seq": peer}, device_id_type=MESH)
+    pl.semaphore_wait(barrier, len(peers))
+
+def remote(src, dst, send, recv, peer):
+    return pltpu.make_async_remote_copy(src_ref=src, dst_ref=dst, send_sem=send, recv_sem=recv,
+        device_id={"seq": peer}, device_id_type=MESH)
+
+def gather_kernel(count, folded, own_ref, all_ref, send_sem, recv_sem):
+    me = lax.axis_index("seq")
+    place = ring_place(me, count, folded)
+    at = lambda offset: ring_index(lax.rem(place + offset + count, count), count, folded)
+    peers = (at(1), at(-1))
+    greet(peers)
+    rows = own_ref.shape[0]
+    steps = count // 2
+    copies = []
+    for step in range(steps):
+        for way in (0, 1):
+            origin = at(-step if way == 0 else step)
+            part = pl.ds(way * (rows // 2), rows // 2) if step == steps - 1 else pl.ds(0, rows)
+            if step:
+                copies[2 * (step - 1) + way].wait_recv()
+            src = all_ref.at[origin, part] if step else own_ref.at[part]
+            copy = remote(src, all_ref.at[origin, part], send_sem.at[way, step], recv_sem.at[way, step], peers[way])
+            copy.start()
+            copies.append(copy)
+        if step == 0:
+            all_ref[me] = own_ref[...]
+    for copy in copies[-2:]:
+        copy.wait_recv()
+    for copy in copies:
+        copy.wait_send()
+
+def ring_gather(own, folded, cid):
+    count = lax.axis_size("seq")
+    steps = count // 2
+    return pl.pallas_call(functools.partial(gather_kernel, count, folded),
+        out_shape=jax.ShapeDtypeStruct((count,) + own.shape, own.dtype),
+        in_specs=[pl.BlockSpec(memory_space=pltpu.VMEM)],
+        out_specs=pl.BlockSpec(memory_space=pltpu.VMEM),
+        scratch_shapes=[pltpu.SemaphoreType.DMA((2, steps)), pltpu.SemaphoreType.DMA((2, steps))],
+        compiler_params=pltpu.CompilerParams(collective_id=cid, has_side_effects=True))(own)
+
+def scatter_kernel(count, folded, part_ref, out_ref, held, send_sem, recv_sem):
+    me = lax.axis_index("seq")
+    place = ring_place(me, count, folded)
+    at = lambda offset: ring_index(lax.rem(place + offset + count, count), count, folded)
+    peers = (at(1), at(-1))
+    greet(peers)
+    rows = part_ref.shape[1]
+    half = rows // 2
+    steps = count // 2
+    copies = []
+    for step in range(steps):
+        for way in (0, 1):
+            goal = at((steps - step) * (1 if way == 0 else -1))
+            whole = pl.ds(way * half, half) if step == 0 else pl.ds(0, rows)
+            if step == 0:
+                src = part_ref.at[goal, whole]
+            else:
+                copies[2 * (step - 1) + way].wait_recv()
+                src = held.at[way, step - 1]
+                if step == 1:
+                    mine, other = pl.ds(way * half, half), pl.ds((1 - way) * half, half)
+                    held[way, 0, mine] = (held[way, 0, mine].astype(jnp.float32) + part_ref[goal, mine].astype(jnp.float32)).astype(held.dtype)
+                    held[way, 0, other] = part_ref[goal, other]
+                else:
+                    held[way, step - 1] = (held[way, step - 1].astype(jnp.float32) + part_ref[goal].astype(jnp.float32)).astype(held.dtype)
+            copy = remote(src, held.at[way, step, whole], send_sem.at[way, step], recv_sem.at[way, step], peers[way])
+            copy.start()
+            copies.append(copy)
+    for copy in copies[-2:]:
+        copy.wait_recv()
+    out_ref[...] = part_ref[me].astype(jnp.float32) + held[0, steps - 1].astype(jnp.float32) + held[1, steps - 1].astype(jnp.float32)
+    for copy in copies:
+        copy.wait_send()
+
+def ring_scatter(parts, folded, cid):
+    count = lax.axis_size("seq")
+    steps = count // 2
+    rows, width = parts.shape[1:]
+    return pl.pallas_call(functools.partial(scatter_kernel, count, folded),
+        out_shape=jax.ShapeDtypeStruct((rows, width), jnp.float32),
+        in_specs=[pl.BlockSpec(memory_space=pltpu.VMEM)],
+        out_specs=pl.BlockSpec(memory_space=pltpu.VMEM),
+        scratch_shapes=[pltpu.VMEM((2, steps, rows, width), parts.dtype),
+            pltpu.SemaphoreType.DMA((2, steps)), pltpu.SemaphoreType.DMA((2, steps))],
+        compiler_params=pltpu.CompilerParams(collective_id=cid, has_side_effects=True, vmem_limit_bytes=40 << 20))(parts)
+
+
+def exchanged(value):
+    return lax.ppermute(value, "pipe", [(0, 1), (1, 0)])
+
+
+def experts_by_rings(local, route_rows, route_scale, moe_gain, gate_up, down_proj, folded):
+    tok_count, width = local.shape
+    seq_count = lax.axis_size("seq")
+    per_device = gate_up.shape[0]
+    own_experts = per_device // 2
+    normed = rms_scale(local, moe_gain)
+    named = route_rows[:, :, None] == jnp.arange(E, dtype=jnp.int32)[None, None, :]
+    dense = jnp.sum(jnp.where(named, route_scale[:, :, None], 0.0), axis=1).astype(jnp.bfloat16)
+    filler = jnp.zeros((tok_count, -(width + E) % 128), jnp.bfloat16)
+    gathered = ring_gather(jnp.concatenate([normed, dense, filler], axis=1), folded, 0)
+    rows = gathered[:, :, :width]
+    scales = lax.dynamic_slice_in_dim(
+        gathered[:, :, width : width + E], lax.axis_index("seq") * own_experts, own_experts, axis=2
+    ).transpose(0, 2, 1)
+    present = scales > 0
+    before = (
+        jnp.arange(tok_count, dtype=jnp.int32)[:, None]
+        < jnp.arange(tok_count, dtype=jnp.int32)[None, :]
+    ).astype(jnp.bfloat16)
+    earlier = jnp.einsum(
+        "neu,ut->net", present.astype(jnp.bfloat16), before, preferred_element_type=jnp.float32
+    ).astype(jnp.int32)
+    slot = jnp.where(present, earlier, -1)
+    taken = slot[:, :, None, :] == jnp.arange(CAP, dtype=jnp.int32)[None, None, :, None]
+    select = jnp.repeat(taken.astype(jnp.bfloat16), 2, axis=1)
+    received = jnp.einsum(
+        "npct,ntd->npcd", select, rows, preferred_element_type=jnp.float32
+    ).astype(jnp.bfloat16)
+    projected = jnp.einsum("spcd,pdh->spch", received, gate_up, preferred_element_type=jnp.float32)
+    half = projected.shape[-1] // 2
+    gate_part = projected[..., :half]
+    up_part = projected[..., half:]
+    hidden = (gate_part * jax.nn.sigmoid(1.702 * gate_part) * (up_part + 1.0)).astype(jnp.bfloat16)
+    partial_value = jnp.einsum(
+        "spch,phd->spcd", hidden, down_proj, preferred_element_type=jnp.float32
+    )
+    finished = (
+        partial_value.reshape(seq_count, own_experts, 2, CAP, width)
+        .sum(axis=2)
+        .astype(jnp.bfloat16)
+        .reshape(seq_count, own_experts * CAP, width)
+    )
+    combine = jnp.where(taken, scales[:, :, None, :], 0).astype(jnp.bfloat16)
+    parts = jnp.einsum(
+        "nkt,nkd->ntd",
+        combine.reshape(seq_count, own_experts * CAP, tok_count),
+        finished,
+        preferred_element_type=jnp.float32,
+    ).astype(jnp.bfloat16)
+    weighted = ring_scatter(parts, folded, 1)
+    return (local.astype(jnp.float32) + weighted).astype(jnp.bfloat16)
+
+
+def split_body(
+    folded,
+    tokens,
+    routes,
+    route_weights,
+    moe_gain,
+    gate_up,
+    down_proj,
+    attn_gain,
+    qkv_proj,
+    head_sink_logits,
+    out_proj,
+):
+    seq_count = lax.axis_size("seq")
+    seq_index = lax.axis_index("seq")
+    pipe_index = lax.axis_index("pipe")
+    query_width = QUERY_HEADS * HEAD_SIZE
+    kv_width = KEY_VALUE_HEADS * HEAD_SIZE
+    share = out_proj.shape[0] // 2
+    own_heads = QUERY_HEADS // 2
+    query_part = lax.dynamic_index_in_dim(
+        qkv_proj[:, :query_width].reshape(qkv_proj.shape[0], seq_count, 2, share),
+        pipe_index,
+        axis=2,
+        keepdims=False,
+    ).reshape(qkv_proj.shape[0], query_width // 2)
+    qkv_part = jnp.concatenate([query_part, qkv_proj[:, query_width:]], axis=1)
+    out_part = lax.dynamic_slice_in_dim(out_proj, pipe_index * share, share, axis=0)
+    qkv_whole = lax.all_gather(qkv_part, "seq", axis=0, tiled=True)
+    out_whole = lax.all_gather(out_part, "seq", axis=0, tiled=True)
+    sinks = lax.dynamic_index_in_dim(
+        head_sink_logits.reshape(seq_count, 2, share // HEAD_SIZE),
+        pipe_index,
+        axis=1,
+        keepdims=False,
+    ).reshape(KEY_VALUE_HEADS, own_heads // KEY_VALUE_HEADS, 1, 1)
+
+    hidden = experts_by_rings(
+        tokens[0], routes[0], route_weights[0], moe_gain, gate_up, down_proj, folded
+    )
+    tok_count, width = hidden.shape
+    normed = rms_scale(hidden, attn_gain)
+    other = exchanged(normed)
+    first = pipe_index == 0
+    both = jnp.concatenate(
+        [jnp.where(first, normed, other), jnp.where(first, other, normed)], axis=0
+    )
+    packed = jnp.dot(both, qkv_whole, preferred_element_type=jnp.float32).astype(jnp.bfloat16)
+    packed = packed.reshape(2, tok_count, query_width // 2 + 2 * kv_width)
+    pairs = packed[:, :, query_width // 2 :]
+    from_left = shifted(pairs[:, tok_count - WINDOW_SPAN :], "seq", 1)
+    halo = jnp.where(seq_index == 0, from_left[:1], from_left)
+    extended = jnp.concatenate([halo, pairs], axis=1)
+    keys = extended[:, :, :kv_width].reshape(2, -1, KEY_VALUE_HEADS, HEAD_SIZE)
+    values = extended[:, :, kv_width:].reshape(2, -1, KEY_VALUE_HEADS, HEAD_SIZE)
+    queries = packed[:, :, : query_width // 2].reshape(
+        2, tok_count, KEY_VALUE_HEADS, own_heads // KEY_VALUE_HEADS, HEAD_SIZE
+    )
+    scores = jnp.einsum(
+        "mqhgd,mkhd->mhgqk", queries, keys, preferred_element_type=jnp.float32
+    ) * (float(HEAD_SIZE) ** (-0.5))
+    query_pos = jnp.arange(tok_count, dtype=jnp.int32)[:, None] + WINDOW_SPAN
+    key_pos = jnp.arange(tok_count + WINDOW_SPAN, dtype=jnp.int32)[None, :]
+    distance = query_pos - key_pos
+    inside = (distance >= 0) & (distance < WINDOW_SPAN)
+    known = (jnp.arange(2, dtype=jnp.int32) > 0) | (seq_index > 0)
+    allowed = inside[None] & ((key_pos >= WINDOW_SPAN)[None] | known[:, None, None])
+    weights = jnp.where(allowed[:, None, None], jnp.exp(scores), 0.0)
+    probs = (weights / (jnp.sum(weights, axis=-1, keepdims=True) + jnp.exp(sinks))).astype(
+        jnp.bfloat16
+    )
+    mixed = jnp.einsum("mhgqk,mkhd->mqhgd", probs, values, preferred_element_type=jnp.float32)
+    attended = mixed.astype(jnp.bfloat16).reshape(2 * tok_count, query_width // 2)
+    projected = jnp.dot(attended, out_whole, preferred_element_type=jnp.float32)
+    early, late = projected[:tok_count], projected[tok_count:]
+    given = jnp.where(first, late, early).astype(jnp.bfloat16)
+    kept = jnp.where(first, early, late)
+    total = kept + exchanged(given).astype(jnp.float32)
+    return (hidden.astype(jnp.float32) + total).astype(jnp.bfloat16)[None]
+
+
 def solution(mesh):
     in_specs = (
         P("pipe", ("groups", "seq"), None),
@@ -177,4 +426,14 @@
         P("seq", None),
     )
     out_specs = P("pipe", ("groups", "seq"), None)
-    return jax.shard_map(body, mesh=mesh, in_specs=in_specs, out_specs=out_specs, check_vma=False)
+    seq_count, pipe_count = mesh.shape["seq"], mesh.shape["pipe"]
+    split = (
+        pipe_count == 2
+        and seq_count % 2 == 0
+        and 2 * E // seq_count >= 2
+        and QUERY_HEADS % (2 * seq_count) == 0
+    )
+    chosen = functools.partial(split_body, True) if split else body
+    return jax.shard_map(
+        chosen, mesh=mesh, in_specs=in_specs, out_specs=out_specs, check_vma=False
+    )

time: 387 us -> 224 us (0.58)
  waiting for transfers between devices: 289 us -> 11.2 us
  Pallas kernels: 0 us -> 128 us
  starting transfers between devices: 18.7 us -> 3.13 us
  matrix products: 43.3 us -> 37 us
  local copies, waits for them, and re-layouts: 17.5 us -> 23.1 us
    all_to_all x2 -> x0, waiting for transfers between devices: 280 us -> none  [the longest x1 181 us: expert_layer(): lax.all_to_all(outgoing, 'seq', split_axis=0, concat_axis=0, tiled=True)]
    pallas_call x0 -> x2, Pallas kernels: none -> 128 us  [the longest x1 64.6 us: ring_gather(): pl.pallas_call(functools.partial(gather_kernel, count, folded), out_shape...]
    all_to_all x2 -> x0, starting transfers between devices: 16.3 us -> none  [the longest x1 8.86 us: expert_layer(): lax.all_to_all(finished, 'seq', split_axis=0, concat_axis=0, tiled=True)]
    dot_general x8, matrix products: 43.3 us -> 37 us  [the longest x1 14.7 us: experts_by_rings(): jnp.einsum('spcd,pdh->spch', received, gate_up, preferred_element_type=jn...]
    unnamed x10 -> x24, local copies, waits for them, and re-layouts: 7.8 us -> 5.47 us
  transfers between devices with their start and end apart: 6 -> 5, of which waited for: 4 -> 3; matrix products, arithmetic and copies ran while one was open for 15% -> 26% of each run, Pallas kernels for 0% -> 58%
where the time goes in v1:
time: 224 us; the launch traced here: 223 us
  Pallas kernels  128 us (57%)
  matrix products  37 us (17%)
  local copies, waits for them, and re-layouts  23.1 us (10%)
  between operations  13.8 us (6%)
  waiting for transfers between devices  11.2 us (5%)
  other arithmetic  6.58 us (3%)
  starting transfers between devices  3.13 us (1%)
    pallas_call x1, Pallas kernels, ring_gather(): pl.pallas_call(functools.partial(gather_kernel, count, folded), out_shape...  64.6 us
    pallas_call x1, Pallas kernels, ring_scatter(): pl.pallas_call(functools.partial(scatter_kernel, count, folded), out_shap...  63.7 us
    dot_general x1, matrix products, experts_by_rings(): jnp.einsum('spcd,pdh->spch', received, gate_up, preferred_element_type=jn...  14.7 us
    dot_general x1, matrix products, experts_by_rings(): jnp.einsum('spch,phd->spcd', hidden, down_proj, preferred_element_type=jn...  10.8 us
    ppermute x1, waiting for transfers between devices, shifted(): return lax.ppermute(value, axis, pairs)  7.78 us
    unnamed x24, local copies, waits for them, and re-layouts  5.47 us
  transfers between devices with their start and end apart: 5, of which 3 were waited for; matrix products, arithmetic and copies ran while one was open for 26% of the time, Pallas kernels for 58%

profile of v1, /device:TPU:0, one launch (start us, length us, event | category | flops | bytes accessed | tf_op | source)
XLA Modules:
  0.0 223.2 jit_solution(4899985483039298354)
XLA Ops:
  6.5 1.3 slice.43
  7.9 0.4 reshape.150
  8.3 2.2 dynamic-slice_reduce_fusion
  10.6 0.9 maximum_bitcast_fusion
  11.5 0.2 all-gather.4.cloned.1.call-start
  11.7 0.8 constant_dynamic-slice_fusion
  12.5 0.2 copy.101
  12.7 0.2 fusion.32
  12.9 0.1 copy.102
  13.1 0.2 fusion.34
  13.2 0.9 concatenate.12.own_ref
  14.1 64.6 %shard_map.100 = bf16[8,128,1536]{2,1,0:T(8,128)(2,1)} custom-call(bf16[128,1536]{1,0:T(8,128)(2,1)} %concatenate.12.own_ref), custom_call_target="tpu_custom_call" | custom-call | tf_op jit(solution)/shard_map/pallas_call | solution.py:223
  78.7 1.9 slice.39
  80.7 1.9 broadcast_compare_fusion
  82.6 1.1 copy.103
  83.7 0.1 fusion.50
  83.8 1.0 copy.104
  84.8 2.0 convert_select_fusion
  86.8 1.2 copy.105
  88.1 0.8 broadcast_in_dim.89
  88.9 14.7 %fusion.4 = f32[8,4,48,1440]{3,2,0,1:T(8,128)} fusion(bf16[4,1440,1440]{2,1,0:T(8,128)(2,1)} %param.14, bf16[8,4,48,128]{3,2,0,1:T(8,128)(2,1)} %bitcast.106, bf16[8,128,1536]{2,1,0:T(8,128)(2,1)S(1)} %copy-done.2), kind=kOutput, calls=%fused_computation.5 | convolution fusion | flops 6938542080 | bytes 28975104 | tf_op jit(solution)/shard_map/spcd,pdh->spch/dot_general | solution.py:309
  103.6 10.8 %bitcast_reduce_fusion = bf16[8,2,48,1440]{3,2,0,1:T(8,128)(2,1)S(1)} fusion(bf16[4,720,1440]{2,1,0:T(8,128)(2,1)} %param.15, f32[8,4,48,1440]{3,2,0,1:T(8,128)} %fusion.4), kind=kOutput, calls=%fused_computation.2 | convolution fusion | flops 3195002880 | bytes 19353600 | tf_op jit(solution)/shard_map/spch,phd->spcd/dot_general | solution.py:314
  114.4 0.1 copy.106
  114.6 0.2 copy.109
  114.8 0.1 fusion.44
  115.0 2.7 %convolution_convert_fusion = bf16[8,128,1440]{1,2,0:T(8,128)(2,1)} fusion(bf16[8,96,128]{2,1,0:T(8,128)(2,1)S(1)} %fusion.44, bf16[8,96,1440]{2,1,0:T(8,128)(2,1)S(1)} %bitcast.99), kind=kOutput, calls=%fused_computation.12 | convolution fusion | flops 284590080 | bytes 5357568 | tf_op jit(solution)/shard_map/nkt,nkd->ntd/dot_general | solution.py:324
  117.7 3.2 %copy.110.part_ref = bf16[8,128,1440]{2,1,0:T(8,128)(2,1)S(1)} copy(bf16[8,128,1440]{1,2,0:T(8,128)(2,1)} %convolution_convert_fusion) | data formatting | bytes 5898240 | tf_op jit(solution)/shard_map/convert_element_type | solution.py:329
  120.9 63.7 %shard_map.101 = f32[128,1440]{1,0:T(8,128)S(1)} custom-call(bf16[8,128,1440]{2,1,0:T(8,128)(2,1)S(1)} %copy.110.part_ref), custom_call_target="tpu_custom_call" | custom-call | tf_op jit(solution)/shard_map/pallas_call | solution.py:268
  184.6 0.2 fusion.28
  184.8 0.2 fusion.30
  185.2 1.6 collective-permute-done
  186.8 0.3 broadcast_select_fusion.1
  187.1 5.1 %reshape.160 = bf16[1440,1536]{1,0:T(8,128)(2,1)} reshape(bf16[8,180,1536]{2,1,0:T(8,128)(2,1)} %all-gather.6.cloned.1.call-done) | data formatting | bytes 8847360
  192.2 3.6 %convolution_convert_fusion.1 = bf16[256,1536]{1,0:T(8,128)(2,1)S(1)} fusion(bf16[1440,1536]{1,0:T(8,128)(2,1)} %reshape.160, bf16[128,1440]{1,0:T(8,128)(2,1)S(1)} %get-tuple-element.10, bf16[128,1440]{1,0:T(8,128)(2,1)S(1)} %get-tuple-element.9), kind=kOutput, calls=%fused_computation.17 | convolution fusion | flops 1134329856 | bytes 5947392 | tf_op jit(solution)/shard_map/dot_general | solution.py:381
  195.9 2.8 %collective-permute-start.1 = (bf16[2,128,512]{2,1,0:T(8,128)(2,1)S(1)}, bf16[2,128,512]{2,1,0:T(8,128)(2,1)S(1)}, u32[]{:S(2)}, u32[]{:S(2)}) collective-permute-start(bf16[2,128,512]{2,1,0:T(8,128)(2,1)S(1)} %slice.54), channel_id=1, source_target_pairs={{0,2},{2,4},{4,6},{6,8},{8,10},{10,12},{12,14},{14,0},{1,3},{3,5},... | collective-permute-start | bytes 786440 | tf_op jit(solution)/shard_map/ppermute | solution.py:31
  198.7 0.1 reshape.156
  198.9 0.1 broadcast_and_fusion
  199.1 0.3 copy.114
  199.4 7.8 %collective-permute-done.1 = bf16[2,128,512]{2,1,0:T(8,128)(2,1)S(1)} collective-permute-done((bf16[2,128,512]{2,1,0:T(8,128)(2,1)S(1)}, bf16[2,128,512]{2,1,0:T(8,128)(2,1)S(1)}, u32[]{:S(2)}, u32[]{:S(2)}) %collective-permute-start.1) | collective-permute-done | bytes 262176 | tf_op jit(solution)/shard_map/ppermute | solution.py:31
  207.3 0.1 copy.113
  207.4 0.1 copy.112
  207.6 1.1 fusion.10
  208.7 1.1 fusion.27
  209.8 0.5 copy.116
  210.4 2.9 %fusion.39 = f32[256,1440]{1,0:T(8,128)S(1)} fusion(bf16[1024,1440]{0,1:T(8,128)(2,1)} %all-gather.4.cloned.1.call-done, bf16[128,8,2,128]{3,2,1,0:T(2,128)(2,1)S(1)} %bitcast.105), kind=kOutput, calls=%fused_computation.43 | convolution fusion | flops 754974720 | bytes 4947968 | tf_op jit(solution)/shard_map/dot_general | solution.py:407
  213.5 1.7 collective-permute-done.2
  215.2 0.2 fusion.42
  215.4 0.9 copy.119
  (53 shorter events, 1.1 us)
Async XLA Ops:
  6.5 5.2 %copy-start = (bf16[256,1440]{0,1:T(8,128)(2,1)S(1)}, bf16[256,1440]{0,1:T(8,128)(2,1)}, u32[]{:S(2)}) copy-start(bf16[256,1440]{0,1:T(8,128)(2,1)} %param.19) | copy-start | bytes 2211844
  6.5 4.0 %slice-start = ((bf16[180,2560]{1,0:T(8,128)(2,1)}), bf16[180,512]{1,0:T(8,128)(2,1)S(1)}, s32[]{:S(2)}) async-start(bf16[180,2560]{1,0:T(8,128)(2,1)} %param.17), calls=%async_computation.2 | async-start | bytes 376832 | tf_op jit(solution)/shard_map/slice | solution.py:360
  6.5 180.5 %all-gather.6.cloned.1.call-start = ((), (), s32[]{:S(2)}) async-start(), calls=%async_computation.1 | async-start | bytes 5087232 | tf_op jit(solution)/shard_map/all_gather | solution.py:362
  6.5 6.0 %copy-start.4 = (bf16[1,128,1440]{1,2,0:T(8,128)(2,1)S(1)}, bf16[1,128,1440]{1,2,0:T(8,128)(2,1)}, u32[]{:S(2)}) copy-start(bf16[1,128,1440]{1,2,0:T(8,128)(2,1)} %param.10) | copy-start | bytes 1105924
  7.8 5.1 %copy-start.7 = (f32[1,128,4]{1,2,0:T(4,128)S(1)}, f32[1,128,4]{1,2,0:T(4,128)}, u32[]{:S(2)}) copy-start(f32[1,128,4]{1,2,0:T(4,128)} %param.12) | copy-start | bytes 6148
  7.9 5.0 %copy-start.8 = (s32[1,128,4]{1,2,0:T(4,128)S(1)}, s32[1,128,4]{1,2,0:T(4,128)}, u32[]{:S(2)}) copy-start(s32[1,128,4]{1,2,0:T(4,128)} %param.11) | copy-start | bytes 6148
  7.9 5.2 %copy-start.6 = (f32[1440]{0:T(1024)S(1)}, f32[1440]{0:T(1024)}, u32[]{:S(2)}) copy-start(f32[1440]{0:T(1024)} %param.13) | copy-start | bytes 17284
  11.5 198.9 %all-gather.4.cloned.1.call-start = ((), (), s32[]{:S(2)}) async-start(), calls=%async_computation | async-start | bytes 3317760 | tf_op jit(solution)/shard_map/all_gather | solution.py:363
  78.7 10.2 %copy-start.2 = (bf16[8,128,1536]{2,1,0:T(8,128)(2,1)S(1)}, bf16[8,128,1536]{2,1,0:T(8,128)(2,1)}, u32[]{:S(2)}) copy-start(bf16[8,128,1536]{2,1,0:T(8,128)(2,1)} %shard_map.100) | copy-start | bytes 9437188
  103.6 10.8 %copy-start.3 = (bf16[8,2,128]{1,2,0:T(8,128)(2,1)S(1)}, bf16[8,2,128]{1,2,0:T(8,128)(2,1)}, u32[]{:S(2)}) copy-start(bf16[8,2,128]{1,2,0:T(8,128)(2,1)} %get-tuple-element.8) | copy-start | bytes 12292
  120.8 64.0 %copy-start.5 = (f32[1440]{0:T(1024)S(1)}, f32[1440]{0:T(1024)}, u32[]{:S(2)}) copy-start(f32[1440]{0:T(1024)} %param.16) | copy-start | bytes 17284
  185.0 1.8 collective-permute-start
  192.2 6.5 %copy-start.9 = (f32[32]{0:T(128)S(1)}, f32[32]{0:T(128)}, u32[]{:S(2)}) copy-start(f32[32]{0:T(128)} %param.18) | copy-start | bytes 388
  195.9 11.3 %collective-permute-start.1 = (bf16[2,128,512]{2,1,0:T(8,128)(2,1)S(1)}, bf16[2,128,512]{2,1,0:T(8,128)(2,1)S(1)}, u32[]{:S(2)}, u32[]{:S(2)}) collective-permute-start(bf16[2,128,512]{2,1,0:T(8,128)(2,1)S(1)} %slice.54), channel_id=1, source_target_pairs={{0,2},{2,4},{4,6},{6,8},{8,10},{10,12},{12,14},{14,0},{1,3},{3,5},... | collective-permute-start | bytes 786440 | tf_op jit(solution)/shard_map/ppermute | solution.py:31
  210.4 5.9 %copy-start.1 = (bf16[256,1440]{0,1:T(8,128)(2,1)S(1)}, bf16[256,1440]{0,1:T(8,128)(2,1)}, u32[]{:S(2)}) copy-start(bf16[256,1440]{0,1:T(8,128)(2,1)} %param.19) | copy-start | bytes 2211844
  213.4 1.8 collective-permute-start.2
Sparse Core Ops, SparseCore 0:
  11.6 94.5 all-gather.5
  108.2 78.4 all-gather.3
